TPU v7x, 256 devices: a whole 4x4x8 slice. The times are simulated.
256 devices in a mesh: row: 16 (over z, x_lo), col: 16 (over y, x_hi, core).
Axes of the slice: x: 4 (x_hi: 2, x_lo: 2; x = x_hi * 2 + x_lo), y: 4, z: 8, core: 2. Of those that a mesh axis runs over, the one named last changes fastest.
Arguments:
- fock_matrix: bfloat16 [12288, 12288], P('row', 'col'), as said below
- density: bfloat16 [12288, 12288], P('row', 'col'), as said below
- intersection: bfloat16 [12288, 12288], P('row', 'col'), as said below
- pattern: int32 [96, 96], replicated, may hold values from 0 to 1, as said below
Outputs:
- gradient_panel: bfloat16 [12288, 2048], P('row', 'col')
Inputs may be any that keep to these rules, and one draw needn't show every extreme that they name: `pattern`: symmetric, with ones on the diagonal; pattern[i, j] is 1 exactly where the centres of blocks i and j lie within the neighbour cutoff of each other. `fock_matrix`: symmetric; zero in every block (i, j) with pattern[i, j] == 0. `density`: symmetric; zero in every block (i, j) with pattern[i, j] == 0. `intersection`: symmetric; zero in every block (i, j) with pattern[i, j] == 0.
All inputs are finite; a program needn't handle non-finite values.
Results may differ from a plain program's by a relative error of at most 0.023.
Values may be sent and summed in bfloat16 or wider, within the bound.
A program may use at most 128 MiB of HBM per device.

v0:
```python
import jax
import jax.numpy as jnp
from jax import lax
from jax.sharding import PartitionSpec as P

BLK = 128


def local(fock_matrix, density, intersection, pattern):
    col_index = lax.axis_index("col")
    tile_rows, tile_cols = fock_matrix.shape
    blocks_col = tile_cols // BLK
    panel_local = jnp.stack([intersection[:, :BLK], fock_matrix[:, :BLK]])
    row_partials = jnp.einsum(
        "ki,skp->sip",
        density,
        lax.all_gather(panel_local, "col", axis=2, tiled=True),
        preferred_element_type=jnp.float32,
    )
    panel_width = row_partials.shape[2]
    owned_blocks = lax.dynamic_slice_in_dim(pattern, col_index * blocks_col, blocks_col, 0)[
        :, ::blocks_col
    ]
    keep_mask = jnp.broadcast_to(
        owned_blocks.astype(jnp.float32)[:, None, :, None],
        (blocks_col, BLK, owned_blocks.shape[1], BLK),
    ).reshape(tile_cols, panel_width)
    combined = lax.psum(row_partials.astype(jnp.bfloat16), "row").astype(jnp.float32)
    filtered = (combined * keep_mask[None]).astype(jnp.bfloat16)
    column_term = jnp.dot(fock_matrix, filtered[0], preferred_element_type=jnp.float32)
    column_term = column_term - jnp.dot(
        intersection, filtered[1], preferred_element_type=jnp.float32
    )
    return lax.psum_scatter(
        column_term.astype(jnp.bfloat16), "col", scatter_dimension=1, tiled=True
    )


def solution(mesh):
    return jax.shard_map(
        local,
        mesh=mesh,
        in_specs=(P("row", "col"), P("row", "col"), P("row", "col"), P()),
        out_specs=P("row", "col"),
        check_vma=False,
    )
```

profile of v0, /device:TPU:1, one launch (start us, length us, event | category | flops | bytes accessed | tf_op | source)
XLA Modules:
  0.0 481.8 jit_solution(13129948686597280517)
XLA Ops:
  6.5 0.0 all-gather.2.cloned.1.call-start
  6.5 1.0 slice.16
  7.6 0.1 copy.14
  7.7 0.9 slice.15
  8.7 0.1 copy.13
  8.8 0.8 pad_maximum_fusion
  9.6 0.0 all-gather.2.cloned.1.call-update
  9.6 0.0 all-reduce.2.cloned.1.call-start
  9.7 73.9 %all-gather.2.cloned.1.call-done = bf16[2,768,2048]{1,2,0:T(8,128)(2,1)} async-done(((bf16[2,768,128]{1,2,0:T(8,128)(2,1)}), bf16[2,768,2048]{1,2,0:T(8,128)(2,1)}) %all-gather.2.cloned.1.call-update) | async-done | bytes 6291472 | tf_op jit(solution)/shard_map/all_gather | solution.py:17
  83.6 9.7 %convert_bitcast_fusion = bf16[2,768,2048]{1,2,0:T(8,128)(2,1)} fusion(bf16[2,768,2048]{1,2,0:T(8,128)(2,1)} %all-gather.2.cloned.1.call-done, bf16[768,768]{1,0:T(8,128)(2,1)S(1)} %copy-done), kind=kOutput, calls=%fused_computation.3 | convolution fusion | flops 4834983936 | bytes 13762560 | tf_op jit(solution)/shard_map/ki,skp->sip/dot_general | solution.py:14
  93.3 0.0 all-reduce.2.cloned.1.call-update
  93.3 0.0 reduce-scatter.2.cloned.1.call-start
  93.4 0.7 constant_dynamic-slice_fusion
  94.1 0.1 slice.17
  94.2 0.5 broadcast_in_dim.2
  94.7 5.6 %copy.17 = f32[96,8,16,128]{3,1,2,0:T(8,128)} copy(f32[96,8,16,128]{3,2,1,0:T(8,128)S(1)} %bitcast.25) | data formatting | bytes 12582912
  100.3 6.6 %copy.11 = f32[768,2048]{0,1:T(8,128)} copy(f32[768,2048]{1,0:T(8,128)} %bitcast.26) | data formatting | bytes 12582912 | tf_op jit(solution)/shard_map/mul | solution.py:29
  106.9 266.3 %all-reduce.2.cloned.1.call-done = bf16[2,768,2048]{1,2,0:T(8,128)(2,1)} async-done(((bf16[2,768,2048]{1,2,0:T(8,128)(2,1)}), bf16[2,768,2048]{1,2,0:T(8,128)(2,1)}) %all-reduce.2.cloned.1.call-update) | async-done | bytes 6291472 | tf_op jit(solution)/shard_map/psum | solution.py:28
  373.2 8.4 %multiply_convert_fusion = bf16[2,768,2048]{1,2,0:T(8,128)(2,1)} fusion(bf16[2,768,2048]{1,2,0:T(8,128)(2,1)} %all-reduce.2.cloned.1.call-done, f32[768,2048]{0,1:T(8,128)} %copy.11), kind=kLoop, calls=%fused_computation | loop fusion | flops 9437184 | bytes 18874368 | tf_op jit(solution)/shard_map/convert_element_type | solution.py:29
  381.6 4.7 fusion
  386.4 4.1 fusion.1
  390.4 0.0 reduce-scatter.2.cloned.1.call-update
  390.5 83.1 %reduce-scatter.2.cloned.1.call-done = bf16[768,128]{0,1:T(8,128)(2,1)} async-done(((bf16[768,2048]{0,1:T(8,128)(2,1)}), bf16[768,128]{0,1:T(8,128)(2,1)}) %reduce-scatter.2.cloned.1.call-update) | async-done | bytes 196624 | tf_op jit(solution)/shard_map/reduce_scatter | solution.py:34
  473.5 1.7 copy.12
  (9 shorter events, 0.0 us)
Async XLA Ops:
  6.5 77.0 %copy-start = (bf16[768,768]{1,0:T(8,128)(2,1)S(1)}, bf16[768,768]{1,0:T(8,128)(2,1)}, u32[]{:S(2)}) copy-start(bf16[768,768]{1,0:T(8,128)(2,1)} %param.5) | copy-start | bytes 3538948
  6.5 77.0 %all-gather.2.cloned.1.call-start = ((), (), s32[]{:S(2)}) async-start(), calls=%async_computation.1 | async-start | bytes 6684672 | tf_op jit(solution)/shard_map/all_gather | solution.py:17
  9.6 363.6 %all-reduce.2.cloned.1.call-start = ((), (), s32[]{:S(2)}) async-start(), calls=%async_computation.2 | async-start | bytes 12582912 | tf_op jit(solution)/shard_map/psum | solution.py:28
  93.3 380.2 %reduce-scatter.2.cloned.1.call-start = ((), (), s32[]{:S(2)}) async-start(), calls=%async_computation.3 | async-start | bytes 3342336 | tf_op jit(solution)/shard_map/reduce_scatter | solution.py:34
  106.9 274.7 %copy-start.2 = (bf16[768,768]{1,0:T(8,128)(2,1)S(1)}, bf16[768,768]{1,0:T(8,128)(2,1)}, u32[]{:S(2)}) copy-start(bf16[768,768]{1,0:T(8,128)(2,1)} %param.4) | copy-start | bytes 3538948
  381.6 4.8 copy-start.1
  381.6 4.8 copy-start.3
Sparse Core Ops, SparseCore 0:
  10.2 73.3 all-gather.1
  93.4 279.7 all-reduce.1
  390.6 82.8 reduce-scatter.1
where the time goes:
time: 482 us
  waiting for transfers between devices  423 us (88%)
  matrix products  18.6 us (4%)
  local copies, waits for them, and re-layouts  17.5 us (4%)
  between operations  13.2 us (3%)
  other arithmetic  9.15 us (2%)
    psum x1, waiting for transfers between devices, local(): lax.psum(row_partials.astype(jnp.bfloat16), 'row').astype(jnp.float32)  266 us
    reduce_scatter x1, waiting for transfers between devices, local(): lax.psum_scatter(column_term.astype(jnp.bfloat16), 'col', scatter_dimensi...  83.1 us
    all_gather x1, waiting for transfers between devices, local(): lax.all_gather(panel_local, 'col', axis=2, tiled=True)  73.9 us
    dot_general x1, matrix products, local(): jnp.einsum('ki,skp->sip', density, lax.all_gather(panel_local, 'col', axi...  9.74 us
  transfers between devices with their start and end apart: 3, of which 3 were waited for; matrix products, arithmetic and copies ran while one was open for 3% of the time, Pallas kernels for 0%

commit v1 on v0

v1 whole, which is shorter than its diff:
```python
import functools

import jax
import jax.numpy as jnp
from jax import lax
from jax.experimental import pallas as pl
from jax.experimental.pallas import tpu as pltpu
from jax.sharding import PartitionSpec as P

BLK = 128
NB = 6
TILE = NB * BLK
HALF = TILE // 2
NQ = 16
NE = NQ * NB
NZ = 8
NY = 4
PER = 4
SLOTS = NZ * PER
MESH = pl.DeviceIdType.MESH
F32 = jnp.float32
BF16 = jnp.bfloat16

OWN_YP, OWN_YM, OWN_X, OWN_C = 0, 2, 4, 6
FWD = 8
PAIR = 16
N_GATHER = 26


def kernel(
    base_ref, pat_s, pat_v, f_hbm, p_hbm, s_hbm, out_ref, most_ref,
    fv, pv, sv, pt, pan, yd, acc, fin, rbuf, xr, yb, zb, gs, gc, rfar, rnear, tx, xg,
    inv, nxt, tab,
    lsem, g_ss, g_rs, a_ss, a_rs, b_ss, b_rs, c_ss, c_rs, d_ss, d_rs,
):
    row, col = lax.axis_index("row"), lax.axis_index("col")
    z, xl = row // 2, row % 2
    y, xh, core = col // 4, (col // 2) % 2, col % 2

    def at_col(yy, xx, cc):
        return yy * 4 + xx * 2 + cc

    up, down, far = (y + 1) % NY, (y + NY - 1) % NY, (y + 2) % NY
    xo, co = 1 - xh, 1 - core
    d_core = (row, at_col(y, xh, co))
    d_x = (row, at_col(y, xo, core))
    d_yp = (row, at_col(up, xh, core))
    d_ym = (row, at_col(down, xh, core))
    d_zp = (((z + 1) % NZ) * 2 + xl, col)
    d_zm = (((z + NZ - 1) % NZ) * 2 + xl, col)
    d_xl = (z * 2 + (1 - xl), col)

    barrier = pltpu.get_barrier_semaphore()
    partners = (d_core, d_x, d_yp, d_ym, d_zp, d_zm, d_xl)
    for d in partners:
        pl.semaphore_signal(barrier, inc=1, device_id=d, device_id_type=MESH)

    loads = [
        pltpu.make_async_copy(p_hbm, pv, lsem.at[0]),
        pltpu.make_async_copy(f_hbm, fv, lsem.at[1]),
        pltpu.make_async_copy(s_hbm, sv, lsem.at[2]),
    ]
    first = pl.ds(0, BLK)
    own = [
        pltpu.make_async_copy(s_hbm.at[:, first], pan.at[0, 0], lsem.at[3]),
        pltpu.make_async_copy(f_hbm.at[:, first], pan.at[0, 1], lsem.at[4]),
    ]
    for c in own + loads:
        c.start()
    pl.semaphore_wait(barrier, len(partners))

    sent = []

    def copy(src, dst, ss, rs, k, dev):
        return pltpu.make_async_remote_copy(
            src_ref=src, dst_ref=dst, send_sem=ss.at[k], recv_sem=rs.at[k], device_id=dev, device_id_type=MESH
        )

    def send(src, dst, ss, rs, k, dev):
        c = copy(src, dst, ss, rs, k, dev)
        c.start()
        sent.append(c)

    def got(dst, ss, rs, k, dev):
        copy(dst, dst, ss, rs, k, dev).wait_recv()

    top, bottom = pl.ds(0, HALF), pl.ds(HALF, HALF)
    s_side, f_side = 0, 1

    def at(dy, dx, dc):
        return dy * 4 + dx * 2 + dc

    def whole(src, dst, k, dev):
        send(pan.at[src], pan.at[dst], g_ss, g_rs, k, dev)

    def part(src, dst, side, k, dev):
        send(pan.at[src, side], pan.at[dst, side], g_ss, g_rs, k, dev)

    def got_whole(dst, k, dev):
        got(pan.at[dst], g_ss, g_rs, k, dev)

    def got_part(dst, side, k, dev):
        got(pan.at[dst, side], g_ss, g_rs, k, dev)

    def give(dy, dx, k):
        whole(at(dy, dx, 0), at(dy, dx, 1), k, d_core)

    def taken(dy, dx, k):
        got_whole(at(dy, dx, 1), k, d_core)

    own[0].wait()
    own[1].wait()
    whole(0, at(3, 0, 0), OWN_YP, d_yp)
    whole(0, at(1, 0, 0), OWN_YM, d_ym)
    whole(0, at(0, 1, 0), OWN_X, d_x)
    give(0, 0, OWN_C)

    base = base_ref[0]
    nxt[NE + 1] = NE
    nxt[NE] = NE

    def count(e, n):
        keep = pat_s[col * NB + e % NB, (e // NB) * NB]
        v = n - base
        ok = (keep > 0) & (v >= 0) & (v < SLOTS)
        inv[e] = jnp.where(ok, v, SLOTS)
        return n + keep

    lax.fori_loop(0, NE, count, jnp.int32(0))

    def back(t, later):
        e = NE - 1 - t
        keep = pat_s[col * NB + e % NB, (e // NB) * NB]
        now = jnp.where(keep > 0, e, later)
        nxt[e] = now
        return now

    lax.fori_loop(0, NE, back, jnp.int32(NE))

    def walk(n, e):
        now = nxt[e]
        tab[n] = now
        return now + 1

    lax.fori_loop(0, NE, walk, jnp.int32(0))

    pat = (pat_v[...] > 0).astype(F32)
    cols = lax.broadcasted_iota(jnp.int32, (NE, NE), 1)
    pat = jnp.where(cols % NB == 0, pat, 0.0)
    grp = lax.broadcasted_iota(jnp.int32, (NQ, NE), 0)
    grp_row = lax.broadcasted_iota(jnp.int32, (NQ, NE), 1) // NB
    counts = jnp.dot(jnp.where(grp == grp_row, 1.0, 0.0), pat, preferred_element_type=F32)
    most_ref[...] = jnp.broadcast_to(
        jnp.max(jnp.sum(counts, axis=1, keepdims=True), axis=0, keepdims=True), most_ref.shape
    )

    fin[pl.ds(SLOTS, 1)] = jnp.zeros((1, BLK, 2 * BLK), BF16)
    yd[pl.ds(NE, 1)] = jnp.zeros((1, BLK, 2 * BLK), BF16)

    loads[0].wait()

    def turn(i, _):
        cols_i = pl.ds(pl.multiple_of(i * BLK, BLK), BLK)
        pt[cols_i, :] = pv[:, cols_i].T
        return 0

    lax.fori_loop(0, NB, turn, 0)

    def products(dy, dx):
        def one(t, _):
            n = at(dy, dx, t)
            q = at_col((y + dy) % NY, (xh + dx) % 2, (core + t) % 2)
            both = jnp.concatenate([pan[n, 0], pan[n, 1]], axis=1)
            r = jnp.dot(pt[...], both, preferred_element_type=F32).astype(BF16)
            yd[pl.ds(q * NB, NB)] = r.reshape(NB, BLK, 2 * BLK)
            return 0

        lax.fori_loop(0, 2, one, 0)

    def from_near(dx, k_lo, k_hi, k_far, k_give):
        got_whole(at(3, dx, 0), k_lo, d_ym)
        part(at(3, dx, 0), at(2, dx, 0), s_side, k_far, d_yp)
        give(3, dx, k_give)
        got_whole(at(1, dx, 0), k_hi, d_yp)
        part(at(1, dx, 0), at(2, dx, 0), f_side, k_far + 1, d_ym)
        give(1, dx, k_give + 1)

    def from_far(dx, k, k_give):
        got_part(at(2, dx, 0), s_side, k, d_ym)
        part(at(2, dx, 0), at(2, dx, 1), s_side, k_give, d_core)
        got_part(at(2, dx, 0), f_side, k + 1, d_yp)
        part(at(2, dx, 0), at(2, dx, 1), f_side, k_give + 1, d_core)

    def taken_far(dx, k):
        got_part(at(2, dx, 1), s_side, k, d_core)
        got_part(at(2, dx, 1), f_side, k + 1, d_core)

    taken(0, 0, OWN_C)
    products(0, 0)
    from_near(0, OWN_YP, OWN_YM, FWD, PAIR)
    got_whole(at(0, 1, 0), OWN_X, d_x)
    whole(at(0, 1, 0), at(3, 1, 0), FWD + 2, d_yp)
    whole(at(0, 1, 0), at(1, 1, 0), FWD + 3, d_ym)
    give(0, 1, PAIR + 2)
    taken(3, 0, PAIR)
    products(3, 0)
    taken(1, 0, PAIR + 1)
    products(1, 0)
    from_far(0, FWD, PAIR + 3)
    taken(0, 1, PAIR + 2)
    products(0, 1)
    taken_far(0, PAIR + 3)
    products(2, 0)
    from_near(1, FWD + 2, FWD + 3, FWD + 4, PAIR + 5)
    taken(3, 1, PAIR + 5)
    products(3, 1)
    taken(1, 1, PAIR + 6)
    products(1, 1)
    from_far(1, FWD + 4, PAIR + 7)
    taken_far(1, PAIR + 7)
    products(2, 1)

    def pack(s, _):
        acc[pl.ds(s, 1)] = yd[pl.ds(tab[base + s], 1)]
        return 0

    lax.fori_loop(0, SLOTS, pack, 0)

    def ring_at(n):
        return (z + n + 2 * NZ) % NZ

    streams = ((0, 0, 4), (1, 1, 4), (0, 1, 3), (1, 0, 3))

    def slots_of(k, h):
        return pl.ds(k * PER + 2 * h, 2)

    def sem_of(d, h, t):
        return (d * 2 + h) * 4 + t

    for t in range(5):
        for d, h, hops in streams:
            u = t - (4 - hops)
            sign = 1 if d == 0 else -1
            to, frm = (d_zp, d_zm) if d == 0 else (d_zm, d_zp)
            if u >= 1:
                k = slots_of(ring_at(sign * (hops - u)), h)
                i = sem_of(d, h, u - 1)
                got(rbuf.at[i], a_ss, a_rs, i, frm)
                acc[k] = (acc[k].astype(F32) + rbuf[i].astype(F32)).astype(BF16)
            if 0 <= u < hops:
                k = slots_of(ring_at(sign * (hops - u)), h)
                i = sem_of(d, h, u)
                send(acc.at[k], rbuf.at[i], a_ss, a_rs, i, to)

    mine = pl.ds(z * PER, PER)
    send(acc.at[mine], xr, d_ss, d_rs, 0, d_xl)
    got(xr, d_ss, d_rs, 0, d_xl)
    fin[mine] = (acc[mine].astype(F32) + xr[...].astype(F32)).astype(BF16)

    for t in range(5):
        for d, h, hops in streams:
            sign = 1 if d == 0 else -1
            to, frm = (d_zp, d_zm) if d == 0 else (d_zm, d_zp)
            k = slots_of(ring_at(-sign * t), h)
            if 1 <= t <= hops:
                got(fin.at[k], b_ss, b_rs, sem_of(d, h, t - 1), frm)
            if t < hops:
                send(fin.at[k], fin.at[k], b_ss, b_rs, sem_of(d, h, t), to)

    loads[1].wait()
    loads[2].wait()

    def pair(n, dy, dx):
        j = ((y + dy) % NY) * 2 + (xh + dx) % 2
        for c in range(2):
            there = pl.ds(c * BLK, BLK)
            q = 2 * j + (core + c) % 2

            def put(i, _, q=q, there=there):
                blk = fin[inv[q * NB + i]]
                rows = pl.ds(pl.multiple_of(i * BLK, BLK), BLK)
                yb[rows, there] = blk[:, :BLK]
                zb[rows, there] = blk[:, BLK:]
                return 0

            lax.fori_loop(0, NB, put, 0)
        g = jnp.dot(fv[...], yb[...], preferred_element_type=F32)
        g = g - jnp.dot(sv[...], zb[...], preferred_element_type=F32)
        gs[n, 0] = g[:, :BLK].astype(BF16)
        gs[n, 1] = g[:, BLK:].astype(BF16)
        cross(n).start()

    def cross(n):
        return copy(gs.at[n, 1], gc.at[n], c_ss, c_rs, n, d_core)

    def join(n):
        cross(n).wait_recv()
        gs[n, 0] = (gs[n, 0].astype(F32) + gc[n].astype(F32)).astype(BF16)

    def far_pair(t, _):
        pair(t, 2, 1 - t)
        return 0

    def near_pair(t, _):
        pair(2 + t, 1 + 2 * (t % 2), 1 - t // 2)
        return 0

    def own_pair(t, _):
        pair(6 + t, 0, 1 - t)
        return 0

    lax.fori_loop(0, 2, far_pair, 0)
    for n in range(2):
        join(n)
        send(gs.at[n, 0, top], rfar.at[2 * n], d_ss, d_rs, 1 + 2 * n, d_yp)
        send(gs.at[n, 0, bottom], rfar.at[2 * n + 1], d_ss, d_rs, 2 + 2 * n, d_ym)
    lax.fori_loop(0, 4, near_pair, 0)
    for n in range(2):
        k = 2 + 2 * n
        join(k)
        got(rfar.at[2 * n], d_ss, d_rs, 1 + 2 * n, d_ym)
        gs[k, 0, top] = (gs[k, 0, top].astype(F32) + rfar[2 * n].astype(F32)).astype(BF16)
        send(gs.at[k, 0], rnear.at[2 * n], d_ss, d_rs, 5 + 2 * n, d_yp)
        k = k + 1
        join(k)
        got(rfar.at[2 * n + 1], d_ss, d_rs, 2 + 2 * n, d_yp)
        gs[k, 0, bottom] = (gs[k, 0, bottom].astype(F32) + rfar[2 * n + 1].astype(F32)).astype(BF16)
        send(gs.at[k, 0], rnear.at[2 * n + 1], d_ss, d_rs, 6 + 2 * n, d_ym)
    lax.fori_loop(0, 2, own_pair, 0)
    for n in range(2):
        join(6 + n)
        got(rnear.at[2 * n], d_ss, d_rs, 5 + 2 * n, d_ym)
        got(rnear.at[2 * n + 1], d_ss, d_rs, 6 + 2 * n, d_yp)
        total = gs[6 + n, 0].astype(F32) + rnear[2 * n].astype(F32) + rnear[2 * n + 1].astype(F32)
        if n == 0:
            tx[...] = total.astype(BF16)
            send(tx, xg, d_ss, d_rs, 9, d_x)
        else:
            out_ref[...] = total
    got(xg, d_ss, d_rs, 9, d_x)
    out_ref[...] += xg[...].astype(F32)

    for c in sent:
        c.wait_send()
    for n in range(NQ // 2):
        cross(n).wait_send()


def one_pass(base, pattern, fock_matrix, density, intersection):
    vmem, dma = pltpu.VMEM, pltpu.SemaphoreType.DMA
    in_vmem = pl.BlockSpec(memory_space=pltpu.VMEM)
    in_smem = pl.BlockSpec(memory_space=pltpu.SMEM)
    raw = pl.BlockSpec(memory_space=pl.ANY)
    tile = vmem((TILE, TILE), BF16)
    return pl.pallas_call(
        kernel,
        out_shape=(
            jax.ShapeDtypeStruct((TILE, BLK), F32),
            jax.ShapeDtypeStruct((8, BLK), F32),
        ),
        in_specs=[in_smem, in_smem, in_vmem, raw, raw, raw],
        out_specs=(in_vmem, in_vmem),
        scratch_shapes=[
            tile, tile, tile, tile,
            vmem((NQ, 2, TILE, BLK), BF16),
            vmem((NE + 1, BLK, 2 * BLK), BF16),
            vmem((SLOTS, BLK, 2 * BLK), BF16),
            vmem((SLOTS + 1, BLK, 2 * BLK), BF16),
            vmem((16, 2, BLK, 2 * BLK), BF16),
            vmem((PER, BLK, 2 * BLK), BF16),
            vmem((TILE, 2 * BLK), BF16),
            vmem((TILE, 2 * BLK), BF16),
            vmem((NQ // 2, 2, TILE, BLK), BF16),
            vmem((NQ // 2, TILE, BLK), BF16),
            vmem((4, HALF, BLK), BF16),
            vmem((4, TILE, BLK), BF16),
            vmem((TILE, BLK), BF16),
            vmem((TILE, BLK), BF16),
            pltpu.SMEM((NE,), jnp.int32),
            pltpu.SMEM((NE + 2,), jnp.int32),
            pltpu.SMEM((NE,), jnp.int32),
            dma((5,)),
            dma((N_GATHER,)), dma((N_GATHER,)),
            dma((16,)), dma((16,)),
            dma((16,)), dma((16,)),
            dma((8,)), dma((8,)),
            dma((10,)), dma((10,)),
        ],
        compiler_params=pltpu.CompilerParams(
            collective_id=0, has_side_effects=True, vmem_limit_bytes=60 * 1024 * 1024
        ),
        name="panel_pass",
    )(base, pattern, pattern, fock_matrix, density, intersection)


def local(fock_matrix, density, intersection, pattern):
    def run(base):
        return one_pass(base.reshape(1), pattern, fock_matrix, density, intersection)

    total, most = run(jnp.int32(0))
    most = most[0, 0].astype(jnp.int32)

    def more(state):
        return state[0] < most

    def again(state):
        base, total = state
        return base + SLOTS, total + run(base)[0]

    _, total = lax.while_loop(more, again, (jnp.int32(SLOTS), total))
    return total.astype(BF16)


def solution(mesh):
    return jax.shard_map(
        local,
        mesh=mesh,
        in_specs=(P("row", "col"), P("row", "col"), P("row", "col"), P()),
        out_specs=P("row", "col"),
        check_vma=False,
    )
```

time: 482 us -> 122 us (0.25)
  waiting for transfers between devices: 423 us -> 0 us
  Pallas kernels: 0 us -> 119 us
  matrix products: 18.6 us -> 0 us
  local copies, waits for them, and re-layouts: 17.5 us -> 1.2 us
  between operations: 13.2 us -> 0.62 us
  other arithmetic: 9.15 us -> 1.69 us
    psum x1 -> x0, waiting for transfers between devices: 266 us -> none  [local(): lax.psum(row_partials.astype(jnp.bfloat16), 'row').astype(jnp.float32)]
    pallas_call x0 -> x1, Pallas kernels: none -> 119 us  [one_pass(): pl.pallas_call(kernel, out_shape=(jax.ShapeDtypeStruct((TILE, BLK), F32),...]
    reduce_scatter x1 -> x0, waiting for transfers between devices: 83.1 us -> none  [local(): lax.psum_scatter(column_term.astype(jnp.bfloat16), 'col', scatter_dimensi...]
    all_gather x1 -> x0, waiting for transfers between devices: 73.9 us -> none  [local(): lax.all_gather(panel_local, 'col', axis=2, tiled=True)]
    dot_general x3 -> x0, matrix products: 18.6 us -> none  [the longest x1 9.74 us: local(): jnp.einsum('ki,skp->sip', density, lax.all_gather(panel_local, 'col', axi...]
    convert_element_type x2 -> x1, other arithmetic: 8.37 us -> 1.69 us  [local(): return total.astype(BF16)]
    mul x1 -> x0, local copies, waits for them, and re-layouts: 6.58 us -> none  [local(): filtered = (combined * keep_mask[None]).astype(jnp.bfloat16)]
    unnamed x11 -> x6, local copies, waits for them, and re-layouts: 5.95 us -> 0.01 us
  transfers between devices with their start and end apart: 3 -> 0, of which waited for: 3 -> 0; matrix products, arithmetic and copies ran while one was open for 3% -> 0% of each run, Pallas kernels for 0% -> 0%
where the time goes in v1:
time: 122 us
  Pallas kernels  119 us (98%)
  other arithmetic  1.69 us (1%)
    pallas_call x1, Pallas kernels, one_pass(): pl.pallas_call(kernel, out_shape=(jax.ShapeDtypeStruct((TILE, BLK), F32),...  119 us

profile of v1, /device:TPU:1, one launch (start us, length us, event | category | flops | bytes accessed | tf_op | source)
XLA Modules:
  0.0 122.3 jit_solution(11428484542622372271)
XLA Ops:
  0.0 0.0 copy-start
  0.0 0.0 copy-start.1
  0.0 0.0 copy-start.2
  0.0 118.6 %panel_pass.2 = (f32[768,128]{1,0:T(8,128)}, f32[8,128]{1,0:T(8,128)}) custom-call(s32[1]{0:T(128)} %constant.2.clone.1.base_ref, s32[96,96]{1,0:T(8,128)} %pat_v.1, s32[96,96]{1,0:T(8,128)} %pat_v.1, bf16[768,768]{1,0:T(8,128)(2,1)} %f_hbm.1, bf16[768,768]{1,0:T(8,128)(2,1)} %p_hbm.1, bf16[768,768]{1,0:T(8,128)(2,1)} %s_hbm.1), custom_call_target="tpu_custom_call" | custom-call | tf_op jit(solution)/shard_map/panel_pass/pallas_call | solution.py:355
  118.6 1.2 slice.3
  120.3 0.0 copy-done
  120.4 0.0 copy-done.1
  120.4 0.0 copy-done.2
  120.4 0.2 while.10
  120.6 1.7 %convert_element_type.11 = bf16[768,128]{1,0:T(8,128)(2,1)} convert(f32[768,128]{1,0:T(8,128)} %get-tuple-element.48) | non-fusion elementwise | flops 98304 | bytes 589824 | tf_op jit(solution)/shard_map/convert_element_type | solution.py:411
Async XLA Ops:
  0.0 120.3 %copy-start = (bf16[768,768]{1,0:T(8,128)(2,1)S(1)}, bf16[768,768]{1,0:T(8,128)(2,1)}, u32[]{:S(2)}) copy-start(bf16[768,768]{1,0:T(8,128)(2,1)} %f_hbm.1) | copy-start | bytes 3538948
  0.0 120.4 %copy-start.1 = (bf16[768,768]{1,0:T(8,128)(2,1)S(1)}, bf16[768,768]{1,0:T(8,128)(2,1)}, u32[]{:S(2)}) copy-start(bf16[768,768]{1,0:T(8,128)(2,1)} %p_hbm.1) | copy-start | bytes 3538948
  0.0 120.4 %copy-start.2 = (bf16[768,768]{1,0:T(8,128)(2,1)S(1)}, bf16[768,768]{1,0:T(8,128)(2,1)}, u32[]{:S(2)}) copy-start(bf16[768,768]{1,0:T(8,128)(2,1)} %s_hbm.1) | copy-start | bytes 3538948

commit v2 on v1

v2 whole, which is shorter than its diff:
```python
import functools

import jax
import jax.numpy as jnp
from jax import lax
from jax.experimental import pallas as pl
from jax.experimental.pallas import tpu as pltpu
from jax.sharding import PartitionSpec as P

BLK = 128
NB = 6
TILE = NB * BLK
HALF = TILE // 2
NQ = 16
NE = NQ * NB
NZ = 8
NY = 4
PER = 4
SLOTS = NZ * PER
MESH = pl.DeviceIdType.MESH
F32 = jnp.float32
BF16 = jnp.bfloat16

OWN_YP, OWN_YM, OWN_X, OWN_C = 0, 1, 2, 3
FWD = 4
PAIR = 10
N_GATHER = 19


def kernel(
    base_ref, pat_hbm, f_hbm, p_hbm, s_hbm, out_ref, most_ref,
    fv, pv, sv, pt, pan, yd0, yd1, acc0, acc1, fin0, fin1, rbuf0, rbuf1, xr0, xr1,
    yb, fy, gs, gc, rfar, rnear, tx, xg,
    pat_s, pat_v, inv, nxt, tab,
    lsem, g_ss, g_rs, a_ss, a_rs, b_ss, b_rs, c_ss, c_rs, d_ss, d_rs, e_ss, e_rs,
):
    yd, acc, fin, rbuf, xr = (yd0, yd1), (acc0, acc1), (fin0, fin1), (rbuf0, rbuf1), (xr0, xr1)
    row, col = lax.axis_index("row"), lax.axis_index("col")
    z, xl = row // 2, row % 2
    y, xh, core = col // 4, (col // 2) % 2, col % 2

    def at_col(yy, xx, cc):
        return yy * 4 + xx * 2 + cc

    up, down, far = (y + 1) % NY, (y + NY - 1) % NY, (y + 2) % NY
    xo, co = 1 - xh, 1 - core
    d_core = (row, at_col(y, xh, co))
    d_x = (row, at_col(y, xo, core))
    d_yp = (row, at_col(up, xh, core))
    d_ym = (row, at_col(down, xh, core))
    d_zp = (((z + 1) % NZ) * 2 + xl, col)
    d_zm = (((z + NZ - 1) % NZ) * 2 + xl, col)
    d_xl = (z * 2 + (1 - xl), col)

    barrier = pltpu.get_barrier_semaphore()
    partners = (d_core, d_x, d_yp, d_ym, d_zp, d_zm, d_xl)
    for d in partners:
        pl.semaphore_signal(barrier, inc=1, device_id=d, device_id_type=MESH)

    loads = [
        pltpu.make_async_copy(p_hbm, pv, lsem.at[0]),
        pltpu.make_async_copy(f_hbm, fv, lsem.at[1]),
        pltpu.make_async_copy(s_hbm, sv, lsem.at[2]),
        pltpu.make_async_copy(pat_hbm, pat_s, lsem.at[5]),
        pltpu.make_async_copy(pat_hbm, pat_v, lsem.at[6]),
    ]
    first = pl.ds(0, BLK)
    own = [
        pltpu.make_async_copy(s_hbm.at[:, first], pan.at[0, 0], lsem.at[3]),
        pltpu.make_async_copy(f_hbm.at[:, first], pan.at[0, 1], lsem.at[4]),
    ]
    for c in own + loads:
        c.start()
    pl.semaphore_wait(barrier, len(partners))

    sent = []

    def copy(src, dst, ss, rs, k, dev):
        return pltpu.make_async_remote_copy(
            src_ref=src, dst_ref=dst, send_sem=ss.at[k], recv_sem=rs.at[k], device_id=dev, device_id_type=MESH
        )

    def send(src, dst, ss, rs, k, dev):
        c = copy(src, dst, ss, rs, k, dev)
        c.start()
        sent.append(c)

    def got(dst, ss, rs, k, dev):
        copy(dst, dst, ss, rs, k, dev).wait_recv()

    top, bottom = pl.ds(0, HALF), pl.ds(HALF, HALF)

    def at(dy, dx, dc):
        return dy * 4 + dx * 2 + dc

    def whole(s, src, dst, k, dev):
        send(pan.at[src, s], pan.at[dst, s], g_ss, g_rs, s * N_GATHER + k, dev)

    def part(s, src, dst, rows, k, dev):
        send(pan.at[src, s, rows], pan.at[dst, s, rows], g_ss, g_rs, s * N_GATHER + k, dev)

    def got_whole(s, dst, k, dev):
        got(pan.at[dst, s], g_ss, g_rs, s * N_GATHER + k, dev)

    def got_part(s, dst, rows, k, dev):
        got(pan.at[dst, s, rows], g_ss, g_rs, s * N_GATHER + k, dev)

    def give(s, dy, dx, k):
        whole(s, at(dy, dx, 0), at(dy, dx, 1), k, d_core)

    def taken(s, dy, dx, k):
        got_whole(s, at(dy, dx, 1), k, d_core)

    def own_y(s):
        whole(s, 0, at(3, 0, 0), OWN_YP, d_yp)
        whole(s, 0, at(1, 0, 0), OWN_YM, d_ym)

    own[0].wait()
    whole(0, 0, at(0, 1, 0), OWN_X, d_x)
    own_y(0)
    give(0, 0, 0, OWN_C)
    own[1].wait()
    whole(1, 0, at(0, 1, 0), OWN_X, d_x)
    give(1, 0, 0, OWN_C)

    base = base_ref[0]
    loads[3].wait()
    loads[4].wait()
    nxt[NE + 1] = NE
    nxt[NE] = NE

    def count(q, n):
        for i in range(NB):
            keep = pat_s[col * NB + i, q * NB]
            v = n - base
            ok = (keep > 0) & (v >= 0) & (v < SLOTS)
            inv[q * NB + i] = jnp.where(ok, v, SLOTS)
            n = n + keep
        return n

    lax.fori_loop(0, NQ, count, jnp.int32(0))

    def back(t, later):
        q = NQ - 1 - t
        for i in reversed(range(NB)):
            later = jnp.where(pat_s[col * NB + i, q * NB] > 0, q * NB + i, later)
            nxt[q * NB + i] = later
        return later

    lax.fori_loop(0, NQ, back, jnp.int32(NE))

    def walk(n, e):
        now = nxt[e]
        tab[n] = now
        return now + 1

    lax.fori_loop(0, NE, walk, jnp.int32(0))

    pat = (pat_v[...] > 0).astype(F32)
    cols = lax.broadcasted_iota(jnp.int32, (NE, NE), 1)
    pat = jnp.where(cols % NB == 0, pat, 0.0)
    grp = lax.broadcasted_iota(jnp.int32, (NQ, NE), 0)
    grp_row = lax.broadcasted_iota(jnp.int32, (NQ, NE), 1) // NB
    counts = jnp.dot(jnp.where(grp == grp_row, 1.0, 0.0), pat, preferred_element_type=F32)
    most_ref[0] = jnp.max(jnp.sum(counts, axis=1, keepdims=True))

    for side in range(2):
        fin[side][pl.ds(SLOTS, 1)] = jnp.zeros((1, BLK, BLK), BF16)
        yd[side][pl.ds(NE, 1)] = jnp.zeros((1, BLK, BLK), BF16)

    loads[0].wait()

    def turn(i, _):
        cols_i = pl.ds(pl.multiple_of(i * BLK, BLK), BLK)
        pt[cols_i, :] = pv[:, cols_i].T
        return 0

    lax.fori_loop(0, NB, turn, 0)

    def products(s, dy, dx):
        n = at(dy, dx, 0)
        both = jnp.concatenate([pan[n, s], pan[n + 1, s]], axis=1)
        r = jnp.dot(pt[...], both, preferred_element_type=F32).astype(BF16)
        for t in range(2):
            q = at_col((y + dy) % NY, (xh + dx) % 2, (core + t) % 2)
            yd[s][pl.ds(q * NB, NB)] = r[:, t * BLK : (t + 1) * BLK].reshape(NB, BLK, BLK)

    def from_near(s, dx, k_lo, k_hi, k_far, k_give):
        got_whole(s, at(3, dx, 0), k_lo, d_ym)
        part(s, at(3, dx, 0), at(2, dx, 0), top, k_far, d_yp)
        give(s, 3, dx, k_give)
        got_whole(s, at(1, dx, 0), k_hi, d_yp)
        part(s, at(1, dx, 0), at(2, dx, 0), bottom, k_far + 1, d_ym)
        give(s, 1, dx, k_give + 1)

    def from_x(s):
        got_whole(s, at(0, 1, 0), OWN_X, d_x)
        whole(s, at(0, 1, 0), at(3, 1, 0), FWD + 2, d_yp)
        whole(s, at(0, 1, 0), at(1, 1, 0), FWD + 3, d_ym)
        give(s, 0, 1, PAIR + 2)

    def from_far(s, dx, k, k_give):
        got_part(s, at(2, dx, 0), top, k, d_ym)
        part(s, at(2, dx, 0), at(2, dx, 1), top, k_give, d_core)
        got_part(s, at(2, dx, 0), bottom, k + 1, d_yp)
        part(s, at(2, dx, 0), at(2, dx, 1), bottom, k_give + 1, d_core)

    def near_0(s):
        from_near(s, 0, OWN_YP, OWN_YM, FWD, PAIR)

    def near_1(s):
        from_near(s, 1, FWD + 2, FWD + 3, FWD + 4, PAIR + 5)

    def far_0(s):
        from_far(s, 0, FWD, PAIR + 3)

    def far_1(s):
        from_far(s, 1, FWD + 4, PAIR + 7)

    def products_own(s):
        taken(s, 0, 0, OWN_C)
        products(s, 0, 0)

    def products_near(s, dx, k):
        taken(s, 3, dx, k)
        products(s, 3, dx)
        taken(s, 1, dx, k + 1)
        products(s, 1, dx)

    def products_x(s):
        taken(s, 0, 1, PAIR + 2)
        products(s, 0, 1)

    def products_far(s, dx, k):
        got_part(s, at(2, dx, 1), top, k, d_core)
        got_part(s, at(2, dx, 1), bottom, k + 1, d_core)
        products(s, 2, dx)

    def pack(s):
        def one(i, _):
            acc[s][pl.ds(i, 1)] = yd[s][pl.ds(tab[base + i], 1)]
            return 0

        lax.fori_loop(0, SLOTS, one, 0)

    def ring_at(n):
        return (z + n + 2 * NZ) % NZ

    streams = tuple((d, p, 4 if d == p // 2 else 3) for p, d in ((0, 0), (2, 1), (1, 0), (3, 1), (2, 0), (0, 1), (3, 0), (1, 1)))
    slot_order = (0, 2, 1, 3)

    def slot_of(k, p):
        return pl.ds(k * PER + p, 1)

    def sem_of(s, d, p, t):
        return s * 32 + (d * PER + p) * 4 + t

    def towards(d):
        return (1, d_zp, d_zm) if d == 0 else (-1, d_zm, d_zp)

    def arrived(s, d, p, u, hops):
        sign, _, frm = towards(d)
        k = slot_of(ring_at(sign * (hops - u)), p)
        i = sem_of(0, d, p, u - 1)
        got(rbuf[s].at[i], a_ss, a_rs, sem_of(s, d, p, u - 1), frm)
        acc[s][k] = (acc[s][k].astype(F32) + rbuf[s][pl.ds(i, 1)].astype(F32)).astype(BF16)

    def ring_sum(s, t):
        for d, p, hops in streams:
            u = t - (4 - hops)
            sign, to, _ = towards(d)
            if u >= 1:
                arrived(s, d, p, u, hops)
            if u >= 0:
                k = ring_at(sign * (hops - u)) * PER + p
                send(acc[s].at[k], rbuf[s].at[sem_of(0, d, p, u)], a_ss, a_rs, sem_of(s, d, p, u), to)

    def last_sum(s):
        for p in slot_order:
            for d in range(2):
                hops = 4 if d == p // 2 else 3
                arrived(s, d, p, hops, hops)
            send(acc[s].at[z * PER + p], xr[s].at[p], e_ss, e_rs, s * PER + p, d_xl)

    def crossed_x(s):
        for p in slot_order:
            got(xr[s].at[p], e_ss, e_rs, s * PER + p, d_xl)
            k = slot_of(z, p)
            fin[s][k] = (acc[s][k].astype(F32) + xr[s][pl.ds(p, 1)].astype(F32)).astype(BF16)
            for d in range(2):
                onward(s, d, p, 0)

    def onward(s, d, p, t):
        sign, to, _ = towards(d)
        k = ring_at(-sign * t) * PER + p
        send(fin[s].at[k], fin[s].at[k], b_ss, b_rs, sem_of(s, d, p, t), to)

    def ring_gather(s, t):
        for d, p, hops in streams:
            if t <= hops:
                sign, _, frm = towards(d)
                k = ring_at(-sign * t) * PER + p
                got(fin[s].at[k], b_ss, b_rs, sem_of(s, d, p, t - 1), frm)
            if t < hops:
                onward(s, d, p, t)

    def chip(n):
        dy = jnp.where(n < 2, 2, jnp.where(n < 6, 1 + 2 * (n % 2), 0))
        dx = jnp.where(n < 2, 1 - n, jnp.where(n < 6, 1 - (n - 2) // 2, 7 - n))
        return ((y + dy) % NY) * 2 + (xh + dx) % 2

    def spread(s, n):
        j = chip(n)
        for c in range(2):
            there = pl.ds(c * BLK, BLK)
            q = 2 * j + (core + c) % 2

            def put(i, _, q=q, there=there):
                rows = pl.ds(pl.multiple_of(i * BLK, BLK), BLK)
                yb[rows, there] = fin[s][inv[q * NB + i]]
                return 0

            lax.fori_loop(0, NB, put, 0)

    def with_y(n, _):
        spread(0, n)
        fy[n] = jnp.dot(fv[...], yb[...], preferred_element_type=F32)
        return 0

    def cross(n):
        return copy(gs.at[n, 1], gc.at[n], c_ss, c_rs, n, d_core)

    def with_z(n, _):
        spread(1, n)
        g = fy[n] - jnp.dot(sv[...], yb[...], preferred_element_type=F32)
        gs[n, 0] = g[:, :BLK].astype(BF16)
        gs[n, 1] = g[:, BLK:].astype(BF16)
        cross(n).start()
        return 0

    products_own(0)
    near_0(0)
    from_x(0)
    products_near(0, 0, PAIR)
    far_0(0)
    products_x(0)
    products_far(0, 0, PAIR + 3)
    near_1(0)
    own_y(1)
    from_x(1)
    products_near(0, 1, PAIR + 5)
    far_1(0)
    products_far(0, 1, PAIR + 7)
    pack(0)
    ring_sum(0, 0)
    products_own(1)
    near_0(1)
    ring_sum(0, 1)
    products_near(1, 0, PAIR)
    near_1(1)
    products_x(1)
    ring_sum(0, 2)
    far_0(1)
    products_near(1, 1, PAIR + 5)
    far_1(1)
    products_far(1, 0, PAIR + 3)
    products_far(1, 1, PAIR + 7)
    ring_sum(0, 3)
    pack(1)
    ring_sum(1, 0)
    last_sum(0)
    ring_sum(1, 1)
    crossed_x(0)
    ring_sum(1, 2)
    ring_gather(0, 1)
    ring_sum(1, 3)
    ring_gather(0, 2)
    last_sum(1)
    ring_gather(0, 3)
    crossed_x(1)
    ring_gather(0, 4)
    loads[1].wait()
    lax.fori_loop(0, 3, with_y, 0)
    ring_gather(1, 1)
    lax.fori_loop(3, 6, with_y, 0)
    ring_gather(1, 2)
    lax.fori_loop(6, 8, with_y, 0)
    ring_gather(1, 3)
    ring_gather(1, 4)
    loads[2].wait()

    def join(n):
        cross(n).wait_recv()
        gs[n, 0] = (gs[n, 0].astype(F32) + gc[n].astype(F32)).astype(BF16)

    lax.fori_loop(0, 2, with_z, 0)
    for n in range(2):
        join(n)
        send(gs.at[n, 0, top], rfar.at[2 * n], d_ss, d_rs, 1 + 2 * n, d_yp)
        send(gs.at[n, 0, bottom], rfar.at[2 * n + 1], d_ss, d_rs, 2 + 2 * n, d_ym)
    lax.fori_loop(2, 6, with_z, 0)
    for n in range(2):
        k = 2 + 2 * n
        join(k)
        got(rfar.at[2 * n], d_ss, d_rs, 1 + 2 * n, d_ym)
        gs[k, 0, top] = (gs[k, 0, top].astype(F32) + rfar[2 * n].astype(F32)).astype(BF16)
        send(gs.at[k, 0], rnear.at[2 * n], d_ss, d_rs, 5 + 2 * n, d_yp)
        k = k + 1
        join(k)
        got(rfar.at[2 * n + 1], d_ss, d_rs, 2 + 2 * n, d_yp)
        gs[k, 0, bottom] = (gs[k, 0, bottom].astype(F32) + rfar[2 * n + 1].astype(F32)).astype(BF16)
        send(gs.at[k, 0], rnear.at[2 * n + 1], d_ss, d_rs, 6 + 2 * n, d_ym)
    lax.fori_loop(6, 8, with_z, 0)
    for n in range(2):
        join(6 + n)
        got(rnear.at[2 * n], d_ss, d_rs, 5 + 2 * n, d_ym)
        got(rnear.at[2 * n + 1], d_ss, d_rs, 6 + 2 * n, d_yp)
        total = gs[6 + n, 0].astype(F32) + rnear[2 * n].astype(F32) + rnear[2 * n + 1].astype(F32)
        if n == 0:
            tx[...] = total.astype(BF16)
            send(tx, xg, d_ss, d_rs, 9, d_x)
        else:
            mine_total = total
    got(xg, d_ss, d_rs, 9, d_x)
    out_ref[...] = (mine_total + xg[...].astype(F32)).astype(BF16)

    for c in sent:
        c.wait_send()
    for n in range(NQ // 2):
        cross(n).wait_send()


def one_pass(base, pattern, fock_matrix, density, intersection):
    vmem, dma = pltpu.VMEM, pltpu.SemaphoreType.DMA
    in_vmem = pl.BlockSpec(memory_space=pltpu.VMEM)
    in_smem = pl.BlockSpec(memory_space=pltpu.SMEM)
    raw = pl.BlockSpec(memory_space=pl.ANY)
    tile = vmem((TILE, TILE), BF16)
    return pl.pallas_call(
        kernel,
        out_shape=(
            jax.ShapeDtypeStruct((TILE, BLK), BF16),
            jax.ShapeDtypeStruct((1,), F32),
        ),
        in_specs=[in_smem, raw, raw, raw, raw],
        out_specs=(in_vmem, in_smem),
        scratch_shapes=[
            tile, tile, tile, tile,
            vmem((NQ, 2, TILE, BLK), BF16),
            *[vmem((NE + 1, BLK, BLK), BF16)] * 2,
            *[vmem((SLOTS, BLK, BLK), BF16)] * 2,
            *[vmem((SLOTS + 1, BLK, BLK), BF16)] * 2,
            *[vmem((32, BLK, BLK), BF16)] * 2,
            *[vmem((PER, BLK, BLK), BF16)] * 2,
            vmem((TILE, 2 * BLK), BF16),
            vmem((NQ // 2, TILE, 2 * BLK), F32),
            vmem((NQ // 2, 2, TILE, BLK), BF16),
            vmem((NQ // 2, TILE, BLK), BF16),
            vmem((4, HALF, BLK), BF16),
            vmem((4, TILE, BLK), BF16),
            vmem((TILE, BLK), BF16),
            vmem((TILE, BLK), BF16),
            pltpu.SMEM((NE, NE), jnp.int32),
            vmem((NE, NE), jnp.int32),
            pltpu.SMEM((NE,), jnp.int32),
            pltpu.SMEM((NE + 2,), jnp.int32),
            pltpu.SMEM((NE,), jnp.int32),
            dma((7,)),
            dma((2 * N_GATHER,)), dma((2 * N_GATHER,)),
            dma((64,)), dma((64,)),
            dma((64,)), dma((64,)),
            dma((8,)), dma((8,)),
            dma((10,)), dma((10,)),
            dma((8,)), dma((8,)),
        ],
        compiler_params=pltpu.CompilerParams(
            collective_id=0, has_side_effects=True, vmem_limit_bytes=60 * 1024 * 1024
        ),
        name="panel_pass",
    )(base, pattern, fock_matrix, density, intersection)


def local(fock_matrix, density, intersection, pattern):
    def run(base):
        return one_pass(base.reshape(1), pattern, fock_matrix, density, intersection)

    first, most = run(jnp.int32(0))

    def more(state):
        return state[0].astype(F32) < most[0]

    def again(state):
        base, total = state
        return base + SLOTS, total + run(base)[0].astype(F32)

    def rest():
        return lax.while_loop(more, again, (jnp.int32(SLOTS), first.astype(F32)))[1].astype(BF16)

    return lax.cond(most[0] > SLOTS, rest, lambda: first)


def solution(mesh):
    return jax.shard_map(
        local,
        mesh=mesh,
        in_specs=(P("row", "col"), P("row", "col"), P("row", "col"), P()),
        out_specs=P("row", "col"),
        check_vma=False,
    )
```

time: 122 us -> 109 us (0.89)
  Pallas kernels: 119 us -> 107 us
  other arithmetic: 1.69 us -> 0 us
    pallas_call x1, Pallas kernels: 119 us -> 107 us  [one_pass(): pl.pallas_call(kernel, out_shape=(jax.ShapeDtypeStruct((TILE, BLK), BF16)...]
    convert_element_type x1 -> x0, other arithmetic: 1.69 us -> none  [local(): return total.astype(BF16)]
    unnamed x6 -> x7, local copies, waits for them, and re-layouts: 0.01 us -> 1.63 us
where the time goes in v2:
time: 109 us
  Pallas kernels  107 us (98%)
  local copies, waits for them, and re-layouts  1.63 us (1%)
    pallas_call x1, Pallas kernels, one_pass(): pl.pallas_call(kernel, out_shape=(jax.ShapeDtypeStruct((TILE, BLK), BF16)...  107 us

profile of v2, /device:TPU:1, one launch (start us, length us, event | category | flops | bytes accessed | tf_op | source)
XLA Modules:
  0.0 109.2 jit_solution(10485599848077448735)
XLA Ops:
  0.0 0.0 copy-start.2
  0.0 0.0 copy-start.1
  0.0 0.0 copy-start
  0.0 106.7 %panel_pass.2 = (bf16[768,128]{1,0:T(8,128)(2,1)}, f32[1]{0:T(128)}) custom-call(s32[1]{0:T(128)} %constant.3.clone.1.base_ref, s32[96,96]{1,0:T(8,128)} %pat_hbm.1, bf16[768,768]{1,0:T(8,128)(2,1)} %f_hbm.1, bf16[768,768]{1,0:T(8,128)(2,1)} %p_hbm.1, bf16[768,768]{1,0:T(8,128)(2,1)} %s_hbm.1), custom_call_target="tpu_custom_call" | custom-call | tf_op jit(solution)/shard_map/panel_pass/pallas_call | solution.py:439
  107.3 0.0 copy-done.2
  107.4 0.0 copy-done.1
  107.4 0.0 copy-done
  107.4 0.2 conditional.1
  107.6 1.6 %copy.16 = bf16[768,128]{1,0:T(8,128)(2,1)} copy(bf16[768,128]{1,0:T(8,128)(2,1)} %get-tuple-element.70) | data formatting | bytes 393216
Async XLA Ops:
  0.0 107.3 %copy-start.2 = (bf16[768,768]{1,0:T(8,128)(2,1)S(1)}, bf16[768,768]{1,0:T(8,128)(2,1)}, u32[]{:S(2)}) copy-start(bf16[768,768]{1,0:T(8,128)(2,1)} %s_hbm.1) | copy-start | bytes 3538948
  0.0 107.4 %copy-start.1 = (bf16[768,768]{1,0:T(8,128)(2,1)S(1)}, bf16[768,768]{1,0:T(8,128)(2,1)}, u32[]{:S(2)}) copy-start(bf16[768,768]{1,0:T(8,128)(2,1)} %p_hbm.1) | copy-start | bytes 3538948
  0.0 107.4 %copy-start = (bf16[768,768]{1,0:T(8,128)(2,1)S(1)}, bf16[768,768]{1,0:T(8,128)(2,1)}, u32[]{:S(2)}) copy-start(bf16[768,768]{1,0:T(8,128)(2,1)} %f_hbm.1) | copy-start | bytes 3538948

commit v3 on v2

--- a/solution.py
+++ b/solution.py
@@ -305,8 +305,9 @@
                 onward(s, d, p, t)
 
     def chip(n):
-        dy = jnp.where(n < 2, 2, jnp.where(n < 6, 1 + 2 * (n % 2), 0))
-        dx = jnp.where(n < 2, 1 - n, jnp.where(n < 6, 1 - (n - 2) // 2, 7 - n))
+        r = n % 3
+        dy = jnp.where(n < 6, jnp.where(r < 2, 2 - r, 3), 0)
+        dx = jnp.where(n < 6, 1 - n // 3, 7 - n)
         return ((y + dy) % NY) * 2 + (xh + dx) % 2
 
     def spread(s, n):
@@ -393,36 +394,61 @@
         cross(n).wait_recv()
         gs[n, 0] = (gs[n, 0].astype(F32) + gc[n].astype(F32)).astype(BF16)
 
+    def send_far(g):
+        join(3 * g)
+        send(gs.at[3 * g, 0, top], rfar.at[2 * g], d_ss, d_rs, 1 + 2 * g, d_yp)
+        send(gs.at[3 * g, 0, bottom], rfar.at[2 * g + 1], d_ss, d_rs, 2 + 2 * g, d_ym)
+
+    def near_part(g, up_side, rows, k):
+        n, there = 3 * g + 2 - up_side, rnear.at[2 * g + 1 - up_side, rows]
+        return gs.at[n, 0, rows], there, 5 + 4 * g + k
+
+    def send_near(g, up_side, rows, k):
+        src, dst, k = near_part(g, up_side, rows, k)
+        send(src, dst, d_ss, d_rs, k, d_yp if up_side else d_ym)
+
+    def got_near(g, up_side, rows, k):
+        _, dst, k = near_part(g, up_side, rows, k)
+        got(dst, d_ss, d_rs, k, d_ym if up_side else d_yp)
+
+    def send_near_free(g):
+        join(3 * g + 1)
+        send_near(g, 1, bottom, 0)
+        join(3 * g + 2)
+        send_near(g, 0, top, 1)
+
+    def send_near_tied(g):
+        got(rfar.at[2 * g], d_ss, d_rs, 1 + 2 * g, d_ym)
+        n = 3 * g + 1
+        gs[n, 0, top] = (gs[n, 0, top].astype(F32) + rfar[2 * g].astype(F32)).astype(BF16)
+        send_near(g, 1, top, 2)
+        got(rfar.at[2 * g + 1], d_ss, d_rs, 2 + 2 * g, d_yp)
+        n = 3 * g + 2
+        gs[n, 0, bottom] = (gs[n, 0, bottom].astype(F32) + rfar[2 * g + 1].astype(F32)).astype(BF16)
+        send_near(g, 0, bottom, 3)
+
+    def total_of(g):
+        for up_side, rows, k in ((1, bottom, 0), (0, top, 1), (1, top, 2), (0, bottom, 3)):
+            got_near(g, up_side, rows, k)
+        return gs[6 + g, 0].astype(F32) + rnear[2 * g].astype(F32) + rnear[2 * g + 1].astype(F32)
+
     lax.fori_loop(0, 2, with_z, 0)
-    for n in range(2):
-        join(n)
-        send(gs.at[n, 0, top], rfar.at[2 * n], d_ss, d_rs, 1 + 2 * n, d_yp)
-        send(gs.at[n, 0, bottom], rfar.at[2 * n + 1], d_ss, d_rs, 2 + 2 * n, d_ym)
-    lax.fori_loop(2, 6, with_z, 0)
-    for n in range(2):
-        k = 2 + 2 * n
-        join(k)
-        got(rfar.at[2 * n], d_ss, d_rs, 1 + 2 * n, d_ym)
-        gs[k, 0, top] = (gs[k, 0, top].astype(F32) + rfar[2 * n].astype(F32)).astype(BF16)
-        send(gs.at[k, 0], rnear.at[2 * n], d_ss, d_rs, 5 + 2 * n, d_yp)
-        k = k + 1
-        join(k)
-        got(rfar.at[2 * n + 1], d_ss, d_rs, 2 + 2 * n, d_yp)
-        gs[k, 0, bottom] = (gs[k, 0, bottom].astype(F32) + rfar[2 * n + 1].astype(F32)).astype(BF16)
-        send(gs.at[k, 0], rnear.at[2 * n + 1], d_ss, d_rs, 6 + 2 * n, d_ym)
+    send_far(0)
+    lax.fori_loop(2, 4, with_z, 0)
+    send_near_free(0)
+    lax.fori_loop(4, 6, with_z, 0)
+    send_near_tied(0)
+    send_far(1)
+    send_near_free(1)
     lax.fori_loop(6, 8, with_z, 0)
-    for n in range(2):
-        join(6 + n)
-        got(rnear.at[2 * n], d_ss, d_rs, 5 + 2 * n, d_ym)
-        got(rnear.at[2 * n + 1], d_ss, d_rs, 6 + 2 * n, d_yp)
-        total = gs[6 + n, 0].astype(F32) + rnear[2 * n].astype(F32) + rnear[2 * n + 1].astype(F32)
-        if n == 0:
-            tx[...] = total.astype(BF16)
-            send(tx, xg, d_ss, d_rs, 9, d_x)
-        else:
-            mine_total = total
-    got(xg, d_ss, d_rs, 9, d_x)
-    out_ref[...] = (mine_total + xg[...].astype(F32)).astype(BF16)
+    join(6)
+    tx[...] = total_of(0).astype(BF16)
+    send(tx, xg, d_ss, d_rs, 0, d_x)
+    send_near_tied(1)
+    join(7)
+    total = total_of(1)
+    got(xg, d_ss, d_rs, 0, d_x)
+    out_ref[...] = (total + xg[...].astype(F32)).astype(BF16)
 
     for c in sent:
         c.wait_send()
@@ -470,11 +496,11 @@
             dma((64,)), dma((64,)),
             dma((64,)), dma((64,)),
             dma((8,)), dma((8,)),
-            dma((10,)), dma((10,)),
+            dma((13,)), dma((13,)),
             dma((8,)), dma((8,)),
         ],
         compiler_params=pltpu.CompilerParams(
-            collective_id=0, has_side_effects=True, vmem_limit_bytes=60 * 1024 * 1024
+            collective_id=0, has_side_effects=True, vmem_limit_bytes=67043328
         ),
         name="panel_pass",
     )(base, pattern, fock_matrix, density, intersection)

time: 109 us -> 108 us (level)
  no operation moved by 1% of the time
where the time goes in v3:
time: 108 us
  Pallas kernels  106 us (98%)
  local copies, waits for them, and re-layouts  1.62 us (2%)
    pallas_call x1, Pallas kernels, one_pass(): pl.pallas_call(kernel, out_shape=(jax.ShapeDtypeStruct((TILE, BLK), BF16)...  106 us

profile of v3, /device:TPU:1, one launch (start us, length us, event | category | flops | bytes accessed | tf_op | source)
XLA Modules:
  0.0 108.2 jit_solution(916956524742008462)
XLA Ops:
  0.0 105.7 %panel_pass.2 = (bf16[768,128]{1,0:T(8,128)(2,1)}, f32[1]{0:T(128)}) custom-call(s32[1]{0:T(128)} %constant.3.clone.1.base_ref, s32[96,96]{1,0:T(8,128)} %pat_hbm.1, bf16[768,768]{1,0:T(8,128)(2,1)} %f_hbm.1, bf16[768,768]{1,0:T(8,128)(2,1)} %p_hbm.1, bf16[768,768]{1,0:T(8,128)(2,1)} %s_hbm.1), custom_call_target="tpu_custom_call" | custom-call | tf_op jit(solution)/shard_map/panel_pass/pallas_call | solution.py:465
  106.3 0.2 conditional.1
  106.6 1.6 %copy.16 = bf16[768,128]{1,0:T(8,128)(2,1)} copy(bf16[768,128]{1,0:T(8,128)(2,1)} %get-tuple-element.70) | data formatting | bytes 393216

commit v4 on v3

--- a/solution.py
+++ b/solution.py
@@ -236,12 +236,11 @@
         got_part(s, at(2, dx, 1), bottom, k + 1, d_core)
         products(s, 2, dx)
 
-    def pack(s):
-        def one(i, _):
-            acc[s][pl.ds(i, 1)] = yd[s][pl.ds(tab[base + i], 1)]
-            return 0
-
-        lax.fori_loop(0, SLOTS, one, 0)
+    def pack(s, chunks):
+        for n in chunks:
+            for p in range(PER):
+                i = ring_at(n) * PER + p
+                acc[s][pl.ds(i, 1)] = yd[s][pl.ds(tab[base + i], 1)]
 
     def ring_at(n):
         return (z + n + 2 * NZ) % NZ
@@ -352,8 +351,9 @@
     products_near(0, 1, PAIR + 5)
     far_1(0)
     products_far(0, 1, PAIR + 7)
-    pack(0)
+    pack(0, (4,))
     ring_sum(0, 0)
+    pack(0, (3, -3, 2, -2, 1, -1, 0))
     products_own(1)
     near_0(1)
     ring_sum(0, 1)
@@ -367,8 +367,9 @@
     products_far(1, 0, PAIR + 3)
     products_far(1, 1, PAIR + 7)
     ring_sum(0, 3)
-    pack(1)
+    pack(1, (4,))
     ring_sum(1, 0)
+    pack(1, (3, -3, 2, -2, 1, -1, 0))
     last_sum(0)
     ring_sum(1, 1)
     crossed_x(0)

time: 108 us -> 108 us (level)
  no operation moved by 1% of the time
where the time goes in v4:
time: 108 us
  Pallas kernels  106 us (98%)
  local copies, waits for them, and re-layouts  1.62 us (2%)
    pallas_call x1, Pallas kernels, one_pass(): pl.pallas_call(kernel, out_shape=(jax.ShapeDtypeStruct((TILE, BLK), BF16)...  106 us

profile of v4, /device:TPU:1, one launch (start us, length us, event | category | flops | bytes accessed | tf_op | source)
XLA Modules:
  0.0 108.2 jit_solution(16364934239070555163)
XLA Ops:
  0.0 105.7 %panel_pass.2 = (bf16[768,128]{1,0:T(8,128)(2,1)}, f32[1]{0:T(128)}) custom-call(s32[1]{0:T(128)} %constant.3.clone.1.base_ref, s32[96,96]{1,0:T(8,128)} %pat_hbm.1, bf16[768,768]{1,0:T(8,128)(2,1)} %f_hbm.1, bf16[768,768]{1,0:T(8,128)(2,1)} %p_hbm.1, bf16[768,768]{1,0:T(8,128)(2,1)} %s_hbm.1), custom_call_target="tpu_custom_call" | custom-call | tf_op jit(solution)/shard_map/panel_pass/pallas_call | solution.py:466
  106.4 0.2 conditional.1
  106.6 1.6 %copy.16 = bf16[768,128]{1,0:T(8,128)(2,1)} copy(bf16[768,128]{1,0:T(8,128)(2,1)} %get-tuple-element.70) | data formatting | bytes 393216
